TPU v7x, 32 devices: a whole 2x2x4 slice. The times are simulated.
32 devices in a mesh: task: 4 (over z), feat: 8 (over y, x, core).
Axes of the slice: x: 2, y: 2, z: 4, core: 2. Of those that a mesh axis runs over, the one named last changes fastest.
Arguments:
- inputs: bfloat16 [4, 64, 512, 512], P('task', 'feat'), may hold values from -6 to 6
- context: int32 [4], P('task'), may hold values from 50 to 500, as said below
- sample_mask: int32 [4, 512], P('task'), may hold values from 0 to 1, as said below
- sample_gain: float32 [512], replicated, may hold values from 0.5 to 1.5
- sample_shift: float32 [512], replicated, may hold values from -2 to 2
- sample_project: bfloat16 [512, 1536], replicated, may hold values from -0.25 to 0.25
- sample_output: bfloat16 [512, 512], replicated, may hold values from -1 to 1
- sample_bias: float32 [512], replicated, may hold values from -2 to 2
- feature_gain: float32 [512], replicated, may hold values from 0.5 to 1.5
- feature_shift: float32 [512], replicated, may hold values from -2 to 2
- feature_project: bfloat16 [512, 1536], replicated, may hold values from -0.25 to 0.25
- feature_output: bfloat16 [512, 512], replicated, may hold values from -0.75 to 0.75
- feature_bias: float32 [512], replicated, may hold values from -2 to 2
- dense_gain: float32 [512], replicated, may hold values from 0.5 to 1.5
- dense_shift: float32 [512], replicated, may hold values from -2 to 2
- up_weight: bfloat16 [512, 2048], replicated, may hold values from -0.25 to 0.25
- up_bias: float32 [2048], replicated, may hold values from -2 to 2
- down_weight: bfloat16 [2048, 512], replicated, may hold values from -0.125 to 0.125
- down_bias: float32 [512], replicated, may hold values from -2 to 2
- cotangent: bfloat16 [4, 64, 512, 512], P('task', 'feat'), may hold values from -6 to 6
Outputs:
- output: bfloat16 [4, 64, 512, 512], P('task', 'feat')
- input_grad: float32 [4, 64, 512, 512], P('task', 'feat')
- sample_gain_grad: float32 [512], replicated
- sample_shift_grad: float32 [512], replicated
- sample_project_grad: float32 [512, 1536], replicated
- sample_output_grad: float32 [512, 512], replicated
- sample_bias_grad: float32 [512], replicated
- feature_gain_grad: float32 [512], replicated
- feature_shift_grad: float32 [512], replicated
- feature_project_grad: float32 [512, 1536], replicated
- feature_output_grad: float32 [512, 512], replicated
- feature_bias_grad: float32 [512], replicated
- dense_gain_grad: float32 [512], replicated
- dense_shift_grad: float32 [512], replicated
- up_weight_grad: float32 [512, 2048], replicated
- up_bias_grad: float32 [2048], replicated
- down_weight_grad: float32 [2048, 512], replicated
- down_bias_grad: float32 [512], replicated
Inputs may be any that keep to these rules, and one draw needn't show every extreme that they name: In every draw one task has context 50 and another 500. `sample_mask`: sample 0 of every task is present.
All inputs are finite; a program needn't handle non-finite values.
Results may differ from a plain program's by a relative error of at most 0.015.
Values may be sent and summed in bfloat16 or wider, within the bound.
A program may use at most 384 MiB of HBM per device.

v0:
```python
import jax
import jax.numpy as jnp
from jax import lax
from jax.sharding import PartitionSpec as P

HEADS = 8
HEAD = 64
EPSILON = 1e-05


def norm_apply(token_rows, norm_gain, norm_shift):
    center = token_rows - jnp.mean(token_rows, axis=-1, keepdims=True)
    spread = jnp.mean(center * center, axis=-1, keepdims=True)
    return center * lax.rsqrt(spread + EPSILON) * norm_gain + norm_shift


def attend_block(queries, key_rows, values, visible):
    scores = jnp.einsum(
        "qche,kche->chqk", queries, key_rows, preferred_element_type=jnp.float32
    ) * HEAD ** (-0.5)
    scores = jnp.where(visible, scores, -1e30)
    highest = jnp.max(scores, axis=-1, keepdims=True)
    weights = jnp.exp(scores - highest)
    totals = jnp.sum(weights, axis=-1, keepdims=True)
    shares = (weights / totals).astype(jnp.bfloat16)
    mixed = jnp.einsum("chqk,kche->qche", shares, values, preferred_element_type=jnp.float32)
    return (mixed.astype(jnp.bfloat16), highest[..., 0] + jnp.log(totals[..., 0]))


def attend_back(queries, key_rows, values, visible, log_total, grad_mixed):
    scores = jnp.einsum(
        "qche,kche->chqk", queries, key_rows, preferred_element_type=jnp.float32
    ) * HEAD ** (-0.5)
    scores = jnp.where(visible, scores, -1e30)
    shares = jnp.exp(scores - log_total[..., None])
    grad_values = jnp.einsum(
        "chqk,qche->kche",
        shares.astype(jnp.bfloat16),
        grad_mixed,
        preferred_element_type=jnp.float32,
    )
    grad_shares = jnp.einsum(
        "qche,kche->chqk", grad_mixed, values, preferred_element_type=jnp.float32
    )
    grad_scores = shares * (grad_shares - jnp.sum(shares * grad_shares, axis=-1, keepdims=True))
    low_scores = grad_scores.astype(jnp.bfloat16)
    grad_queries = jnp.einsum(
        "chqk,kche->qche", low_scores, key_rows, preferred_element_type=jnp.float32
    ) * HEAD ** (-0.5)
    grad_keys = jnp.einsum(
        "chqk,qche->kche", low_scores, queries, preferred_element_type=jnp.float32
    ) * HEAD ** (-0.5)
    return jnp.stack([grad_queries, grad_keys, grad_values], axis=2)


def branch_forward(
    hidden, norm_gain, norm_shift, input_weight, output_weight, output_bias, visible
):
    full_shape = hidden.shape
    normed = (
        norm_apply(hidden, norm_gain, norm_shift).astype(jnp.bfloat16).reshape(-1, full_shape[-1])
    )
    packed = jnp.dot(normed, input_weight, preferred_element_type=jnp.float32).astype(jnp.bfloat16)
    packed = packed.reshape(full_shape[:3] + (3, HEADS, HEAD))

    def one_block(block_items):
        return attend_block(block_items[0], block_items[1], block_items[2], block_items[3])

    mixed, log_total = lax.map(
        one_block, (packed[:, :, :, 0], packed[:, :, :, 1], packed[:, :, :, 2], visible)
    )
    mixed_flat = mixed.reshape(-1, full_shape[-1])
    branch = jnp.dot(mixed_flat, output_weight, preferred_element_type=jnp.float32) + output_bias
    return (branch.reshape(full_shape), (normed, packed, mixed_flat, log_total))


def branch_backward(
    hidden, norm_gain, norm_shift, input_weight, output_weight, visible, saved, grad_branch
):
    normed, packed, mixed_flat, log_total = saved
    full_shape = hidden.shape
    low_grad = grad_branch.astype(jnp.bfloat16)
    grad_bias = jnp.sum(low_grad.astype(jnp.float32), axis=0)
    grad_output = jnp.einsum("nd,ne->de", mixed_flat, low_grad, preferred_element_type=jnp.float32)
    grad_mixed = jnp.einsum(
        "ne,de->nd", low_grad, output_weight, preferred_element_type=jnp.float32
    )
    grad_mixed = grad_mixed.astype(jnp.bfloat16).reshape(full_shape[:3] + (HEADS, HEAD))

    def one_block(block_items):
        return attend_back(*block_items)

    grad_packed = lax.map(
        one_block,
        (
            packed[:, :, :, 0],
            packed[:, :, :, 1],
            packed[:, :, :, 2],
            visible,
            log_total,
            grad_mixed,
        ),
    )
    grad_packed = grad_packed.reshape(-1, 3 * full_shape[-1]).astype(jnp.bfloat16)
    grad_input = jnp.einsum("nd,ne->de", normed, grad_packed, preferred_element_type=jnp.float32)
    grad_normed = jnp.einsum(
        "ne,de->nd", grad_packed, input_weight, preferred_element_type=jnp.float32
    )
    token_rows = hidden.reshape(-1, full_shape[-1])
    unused, pullback = jax.vjp(norm_apply, token_rows, norm_gain, norm_shift)
    grad_rows, grad_gain, grad_shift = pullback(grad_normed)
    return (grad_rows, (grad_gain, grad_shift, grad_input, grad_output, grad_bias))


def body(
    inputs,
    context,
    sample_mask,
    sample_gain,
    sample_shift,
    sample_project,
    sample_output,
    sample_bias,
    feature_gain,
    feature_shift,
    feature_project,
    feature_output,
    feature_bias,
    dense_gain,
    dense_shift,
    up_weight,
    up_bias,
    down_weight,
    down_bias,
    cotangent,
):
    task_count, feat_count, sample_count, model_width = inputs.shape
    position = lax.broadcasted_iota(jnp.int32, (task_count, sample_count), 1)
    task_keys = (position < context[:, None]) & (sample_mask == 1)
    pair_keys = jnp.broadcast_to(task_keys[:, None, :], (task_count, feat_count, sample_count))
    pair_keys = pair_keys.reshape(-1, sample_count)
    stream_in = inputs.astype(jnp.float32).reshape(
        task_count * feat_count, sample_count, 1, model_width
    )
    sample_branch, sample_saved = branch_forward(
        stream_in, sample_gain, sample_shift, sample_project, sample_output, sample_bias, pair_keys
    )
    after_sample = (stream_in + sample_branch).reshape(inputs.shape)
    regrouped, grad_result = (
        lax.all_to_all(
            after_sample.astype(jnp.bfloat16), "feat", split_axis=2, concat_axis=1, tiled=True
        ),
        lax.all_to_all(cotangent, "feat", split_axis=2, concat_axis=1, tiled=True),
    )
    middle = regrouped.astype(jnp.float32)
    group_shape = middle.shape
    feature_keys = jnp.ones(group_shape[:2], jnp.bool_)
    feature_branch, feature_saved = branch_forward(
        middle,
        feature_gain,
        feature_shift,
        feature_project,
        feature_output,
        feature_bias,
        feature_keys,
    )
    after_feature = (middle + feature_branch).reshape(-1, model_width)
    dense_in = norm_apply(after_feature, dense_gain, dense_shift).astype(jnp.bfloat16)
    pre_act = jnp.dot(dense_in, up_weight, preferred_element_type=jnp.float32) + up_bias
    activated = jax.nn.gelu(pre_act).astype(jnp.bfloat16)
    result = (
        after_feature
        + jnp.dot(activated, down_weight, preferred_element_type=jnp.float32)
        + down_bias
    )
    output = lax.all_to_all(
        result.reshape(group_shape).astype(jnp.bfloat16),
        "feat",
        split_axis=1,
        concat_axis=2,
        tiled=True,
    )
    grad_low = grad_result.reshape(-1, model_width)
    grad_stream = grad_low.astype(jnp.float32)
    grad_down_bias = jnp.sum(grad_stream, axis=0)
    grad_down = jnp.einsum("nf,nd->fd", activated, grad_low, preferred_element_type=jnp.float32)
    grad_act = jnp.einsum("nd,fd->nf", grad_low, down_weight, preferred_element_type=jnp.float32)
    unused, gelu_pull = jax.vjp(jax.nn.gelu, pre_act)
    grad_pre = gelu_pull(grad_act)[0].astype(jnp.bfloat16)
    grad_up_bias = jnp.sum(grad_pre.astype(jnp.float32), axis=0)
    grad_up = jnp.einsum("nd,nf->df", dense_in, grad_pre, preferred_element_type=jnp.float32)
    grad_dense_in = jnp.einsum("nf,df->nd", grad_pre, up_weight, preferred_element_type=jnp.float32)
    unused_rows, norm_pull = jax.vjp(norm_apply, after_feature, dense_gain, dense_shift)
    grad_norm_rows, grad_dense_gain, grad_dense_shift = norm_pull(grad_dense_in)
    grad_after_feature = grad_stream + grad_norm_rows
    grad_feature_rows, feature_grads = branch_backward(
        middle,
        feature_gain,
        feature_shift,
        feature_project,
        feature_output,
        feature_keys,
        feature_saved,
        grad_after_feature,
    )
    (
        grad_feature_gain,
        grad_feature_shift,
        grad_feature_project,
        grad_feature_output,
        grad_feature_bias,
    ) = feature_grads
    grad_sent = (grad_after_feature + grad_feature_rows).astype(jnp.bfloat16).reshape(group_shape)
    grad_returned = lax.all_to_all(grad_sent, "feat", split_axis=1, concat_axis=2, tiled=True)
    grad_after_sample = grad_returned.astype(jnp.float32).reshape(-1, model_width)
    grad_sample_rows, sample_grads = branch_backward(
        stream_in,
        sample_gain,
        sample_shift,
        sample_project,
        sample_output,
        pair_keys,
        sample_saved,
        grad_after_sample,
    )
    (
        grad_sample_gain,
        grad_sample_shift,
        grad_sample_project,
        grad_sample_output,
        grad_sample_bias,
    ) = sample_grads
    input_grad = (grad_after_sample + grad_sample_rows).reshape(inputs.shape)
    combined = lax.psum(
        (
            grad_sample_gain,
            grad_sample_shift,
            grad_sample_project,
            grad_sample_output,
            grad_sample_bias,
            grad_feature_gain,
            grad_feature_shift,
            grad_feature_project,
            grad_feature_output,
            grad_feature_bias,
            grad_dense_gain,
            grad_dense_shift,
            grad_up,
            grad_up_bias,
            grad_down,
            grad_down_bias,
        ),
        ("task", "feat"),
    )
    return (output, input_grad) + tuple(combined)


def solution(mesh):
    return jax.shard_map(
        body,
        mesh=mesh,
        in_specs=(
            P("task", "feat", None, None),
            P("task"),
            P("task", None),
            P(),
            P(),
            P(),
            P(),
            P(),
            P(),
            P(),
            P(),
            P(),
            P(),
            P(),
            P(),
            P(),
            P(),
            P(),
            P(),
            P("task", "feat", None, None),
        ),
        out_specs=(
            P("task", "feat", None, None),
            P("task", "feat", None, None),
            P(),
            P(),
            P(),
            P(),
            P(),
            P(),
            P(),
            P(),
            P(),
            P(),
            P(),
            P(),
            P(),
            P(),
            P(),
            P(),
        ),
        check_vma=False,
    )
```

profile of v0, /device:TPU:0, one launch (start us, length us, event | category | flops | bytes accessed | tf_op | source)
XLA Modules:
  0.0 1334.4 jit_solution(14459133283832784476)
XLA Ops:
  25.1 16.8 %copy.147 = bf16[4096,1536]{0,1:T(8,128)(2,1)} copy(bf16[4096,1536]{1,0:T(8,128)(2,1)} %convolution_convert_fusion.1) | data formatting | bytes 25165824 | tf_op jit(solution)/shard_map/convert_element_type | solution.py:63
  63.2 90.0 %while.4 = (s32[]{:T(128)}, bf16[8,512,1,8,64]{1,4,3,2,0:T(8,128)(2,1)}, f32[8,1,8,512]{3,2,1,0:T(8,128)}, bf16[8,512,1,8,64]{1,4,3,2,0:T(8,128)(2,1)}, pred[8,5...) while((s32[]{:T(128)}, ...), condition=%wide.region_5.6_spmd, body=%wide.region_2.5_spmd.sunk | while | flops 562294784 | bytes 27399256 | solution.py:69
  185.9 42.5 %all-to-all-done = bf16[1,8,512,512]{3,1,0,2:T(8,128)(2,1)} async-done(((bf16[1,8,512,512]{3,1,0,2:T(8,128)(2,1)}), bf16[1,8,512,512]{3,1,0,2:T(8,128)(2,1)}, u32[]{:S(2)}, u32[]{:S(2)}) %all-to-all-start) | async-done | bytes 4194336 | tf_op jit(solution)/shard_map/all_to_all | solution.py:150
  269.3 30.9 %reshape.577 = bf16[1,64,64,3,8,64]{5,4,3,2,1,0:T(8,128)(2,1)} reshape(bf16[4096,1536]{1,0:T(8,128)(2,1)} %convolution_convert_fusion) | data formatting | bytes 25165824 | tf_op jit(solution)/shard_map/reshape | solution.py:64
  300.2 16.8 %fusion.87 = (bf16[1,64,64,1,8,64]{5,4,3,2,1,0:T(8,128)(2,1)}, bf16[1,64,64,1,8,64]{5,4,3,2,1,0:T(8,128)(2,1)}, bf16[1,64,64,1,8,64]{5,4,3,2,1,0:T(8,128)(2,1)}) fusion(bf16[1,64,64,3,8,64]{5,4,3,2,1,0:T(8,128)(2,1)} %reshape.577), kind=kLoop, calls=%fused_computation.166 | loop fusion | bytes 25165824 | tf_op jit(solution)/shard_map/slice | solution.py:70
  317.0 12.7 copy.199
  329.7 22.7 %multiply_reduce_fusion.2 = (f32[64,8,64]{2,1,0:T(8,128)S(1)}, f32[64,8,64,64]{2,3,1,0:T(8,128)}) fusion(bf16[1,64,64,1,8,64]{5,4,3,2,1,0:T(8,128)(2,1)} %get-tuple-element.260, bf16[1,64,64,1,8,64]{5,4,3,2,1,0:T(8,128)(2,1)} %get-tuple-element.261), kind=kOutput, calls=%fused_computation.82 | convolution fusion | flops 272596992 | bytes 16908288 | tf_op jit(solution)/shard_map/while/body/eval_jaxpr/qche,kche->chqk/dot_general | solution.py:18
  363.6 13.6 %convert_bitcast_fusion = bf16[64,64,8,64]{0,3,2,1:T(8,128)(2,1)} fusion(f32[64,8,64,64]{2,3,1,0:T(8,128)} %get-tuple-element.277, f32[64,8,64]{2,1,0:T(8,128)S(1)} %fusion.57, f32[64,8,64]{2,1,0:T(8,128)S(1)} %get-tuple-element.276, bf16[1,64,64,1,8,64]{1,5,4,2,3,0:T(8,128)(2,1)} %copy.199), kind=kOutput, calls=%fused_computation.121 | convolution fusion | flops 278921216 | bytes 17039360 | tf_op jit(solution)/shard_map/while/body/eval_jaxpr/chqk,kche->qche/dot_general | solution.py:26
  377.2 12.6 copy.158
  420.9 22.4 %multiply_convert_fusion.1 = (bf16[4096,2048]{1,0:T(8,128)(2,1)}, f32[4096,2048]{1,0:T(8,128)}) fusion(f32[2048]{0:T(1024)S(1)} %copy-done.69, bf16[512,2048]{1,0:T(8,128)(2,1)S(1)} %copy-done, f32[4096,512]{1,0:T(8,128)S(1)} %copy-done.7, f32[512]{0:T(512)S(1)} %copy-done.72, f32[512]{0:T(512)S(1)} %copy-done.55, f32[4096]{0:T(1024)S(1)} %fusion.74, ...), kind=kOutput, calls=%fused_computation.71 | convolution fusion | flops 8684306432 | bytes 60862464 | tf_op jit(solution)/shard_map/dot_general | solution.py:169
  443.3 34.8 %convert_reduce_fusion = (f32[2048]{0:T(1024)}, bf16[4096,2048]{1,0:T(8,128)(2,1)}) fusion(f32[4096,2048]{1,0:T(8,128)} %get-tuple-element.281, f32[2048]{0:T(1024)S(1)} %copy-done.69, bf16[4096,512]{1,0:T(8,128)(2,1)} %bitcast.296, bf16[2048,512]{1,0:T(8,128)(2,1)} %param.41), kind=kOutput, calls=%fused_computation.70 | convolution fusion | flops 8782870528 | bytes 56639488 | tf_op jit(solution)/shard_map/nd,fd->nf/dot_general | solution.py:187
  478.1 17.5 %multiply_reduce_fusion.3 = (f32[512]{0:T(512)}, f32[4096]{0:T(1024)S(1)}, f32[512]{0:T(512)}, f32[4096,512]{1,0:T(8,128)}) fusion(f32[4096,512]{1,0:T(8,128)S(1)} %copy-done.7, f32[4096]{0:T(1024)S(1)} %fusion.74, f32[4096]{0:T(1024)S(1)} %broadcast_multiply_fusion.1, f32[512]{0:T(512)S(1)} %copy-done.55, bf16[4096,2048]{1,0:T(8,128)(2,1)} %get-tuple-element.288, ...), kind=kOutput, calls=%fused_computation.103 | convolution fusion | flops 8606707712 | bytes 35706880 | tf_op jit(solution)/shard_map/nf,df->nd/dot_general | solution.py:192
  522.8 12.8 copy.171
  535.6 19.6 %multiply_reduce_fusion.1 = (f32[64,8,64]{2,1,0:T(8,128)S(1)}, f32[64,8,64,64]{2,3,1,0:T(8,128)}) fusion(f32[64,8,64,64]{2,3,1,0:T(8,128)} %get-tuple-element.277, f32[64,8,64]{2,1,0:T(8,128)S(1)} %copy-done.18, bf16[64,64,8,64]{0,3,2,1:T(8,128)(2,1)} %copy.171, bf16[1,64,64,1,8,64]{1,5,4,2,3,0:T(8,128)(2,1)} %copy.199), kind=kOutput, calls=%fused_computation.75 | convolution fusion | flops 276791296 | bytes 25427968 | tf_op jit(solution)/shard_map/while/body/eval_jaxpr/qche,kche->chqk/dot_general | solution.py:42
  555.2 15.0 %multiply_convert_fusion.2 = bf16[64,8,64,64]{2,3,1,0:T(8,128)(2,1)} fusion(f32[64,8,64,64]{2,3,1,0:T(8,128)} %get-tuple-element.284, f32[64,8,64,64]{2,3,1,0:T(8,128)} %get-tuple-element.277, f32[64,8,64]{2,1,0:T(8,128)S(1)} %get-tuple-element.283, f32[64,8,64]{2,1,0:T(8,128)S(1)} %copy-done.18), kind=kLoop, calls=%fused_computation.74 | loop fusion | flops 10485760 | bytes 21233664 | tf_op jit(solution)/shard_map/while/body/eval_jaxpr/convert_element_type | solution.py:46
  570.1 16.3 %multiply_bitcast_fusion.1 = bf16[64,64,1,8,64]{4,0,3,1,2:T(8,128)(2,1)} fusion(bf16[64,8,64,64]{2,3,1,0:T(8,128)(2,1)} %multiply_convert_fusion.2, bf16[1,64,64,1,8,64]{5,4,3,2,1,0:T(8,128)(2,1)} %get-tuple-element.260), kind=kOutput, calls=%fused_computation.73 | convolution fusion | flops 272629760 | bytes 12582912 | tf_op jit(solution)/shard_map/while/body/eval_jaxpr/chqk,kche->qche/dot_general | solution.py:47
  586.4 18.4 %multiply_bitcast_fusion = bf16[64,64,1,8,64]{4,0,3,1,2:T(8,128)(2,1)} fusion(bf16[64,8,64,64]{2,3,1,0:T(8,128)(2,1)} %multiply_convert_fusion.2, bf16[1,64,64,1,8,64]{5,4,3,2,1,0:T(8,128)(2,1)} %get-tuple-element.261), kind=kOutput, calls=%fused_computation.72 | convolution fusion | flops 272629760 | bytes 12582912 | tf_op jit(solution)/shard_map/while/body/eval_jaxpr/chqk,qche->kche/dot_general | solution.py:50
  604.9 13.1 convolution_bitcast_fusion
  618.0 17.4 %maximum_convert_fusion = bf16[64,64,3,8,64]{4,0,3,1,2:T(8,128)(2,1)} fusion(bf16[64,64,1,8,64]{4,0,3,1,2:T(8,128)(2,1)} %convolution_bitcast_fusion, bf16[64,64,1,8,64]{4,0,3,1,2:T(8,128)(2,1)} %multiply_bitcast_fusion, bf16[64,64,1,8,64]{4,0,3,1,2:T(8,128)(2,1)} %multiply_bitcast_fusion.1), kind=kLoop, calls=%fused_computation.60 | loop fusion | flops 12582912 | bytes 25165824 | tf_op jit(solution)/shard_map/convert_element_type | solution.py:104
  635.4 25.0 %copy.174 = bf16[64,64,3,8,64]{4,3,2,1,0:T(8,128)(2,1)} copy(bf16[64,64,3,8,64]{4,0,3,1,2:T(8,128)(2,1)} %maximum_convert_fusion) | data formatting | bytes 25165824 | tf_op jit(solution)/shard_map/convert_element_type | solution.py:104
  660.4 32.6 %convert_element_type.212 = bf16[4096,1536]{1,0:T(8,128)(2,1)} reshape(bf16[64,64,3,8,64]{4,3,2,1,0:T(8,128)(2,1)} %copy.174) | data formatting | bytes 25165824 | tf_op jit(solution)/shard_map/convert_element_type | solution.py:104
  703.5 15.4 %multiply_reduce_fusion.4 = (f32[512]{0:T(512)}, f32[4096]{0:T(1024)S(1)}, f32[512]{0:T(512)}, f32[4096,512]{1,0:T(8,128)}) fusion(f32[1,8,8,64,512]{4,3,1,2,0:T(8,128)} %copy.153, f32[4096]{0:T(1024)S(1)} %copy-done.34, f32[4096]{0:T(1024)S(1)} %copy-done.30, f32[512]{0:T(512)S(1)} %copy-done.48, bf16[4096,1536]{1,0:T(8,128)(2,1)} %convert_element_type.212, ...), kind=kOutput, calls=%fused_computation.106 | convolution fusion | flops 6459223040 | bytes 30988288 | tf_op jit(solution)/shard_map/ne,de->nd/dot_general | solution.py:106
  741.2 15.1 %fusion.93 = f32[2048,512]{1,0:T(8,128)} fusion(bf16[4096,2048]{1,0:T(8,128)(2,1)} %get-tuple-element.280, bf16[4096,512]{1,0:T(8,128)(2,1)} %bitcast.297), kind=kOutput, calls=%fused_computation.172 | convolution fusion | flops 8589934592 | bytes 25165824 | tf_op jit(solution)/shard_map/nf,nd->fd/dot_general | solution.py:186
  756.3 18.0 %add_convert_fusion.3 = bf16[4096,512]{1,0:T(8,128)(2,1)} fusion(f32[4096,512]{1,0:T(8,128)} %copy-done.6, bf16[4096,2048]{1,0:T(8,128)(2,1)} %get-tuple-element.280, bf16[2048,512]{1,0:T(8,128)(2,1)S(1)} %copy-done.62, f32[512]{0:T(512)S(1)} %copy-done.71), kind=kOutput, calls=%fused_computation.118 | convolution fusion | flops 8596226048 | bytes 31459328 | tf_op jit(solution)/shard_map/dot_general | solution.py:173
  774.3 12.6 fusion.91
  790.4 17.0 %fusion.81 = f32[512,2048]{1,0:T(8,128)} fusion(bf16[4096,2048]{1,0:T(8,128)(2,1)} %get-tuple-element.288, f32[4096,512]{1,0:T(8,128)S(1)} %bitcast.292, f32[512]{0:T(512)S(1)} %copy-done.73, f32[512]{0:T(512)S(1)} %copy-done.56, f32[4096]{0:T(1024)S(1)} %copy-done.44, f32[4096]{0:T(1024)S(1)} %copy-done.32), kind=kOutput, calls=%fused_computation.161 | convolution fusion | flops 8600420352 | bytes 29396992 | tf_op jit(solution)/shard_map/nd,nf->df/dot_general | solution.py:191
  842.2 152.8 %while.5 = (s32[]{:T(128)}, bf16[8,512,1,3,8,64]{1,5,4,3,2,0:T(8,128)(2,1)}, bf16[8,512,1,8,64]{1,4,3,2,0:T(8,128)(2,1)}, pred[8,512]{1,0:T(8,128)(4,1)S(1)}, bf...) while((s32[]{:T(128)}, ...), condition=%wide.region_19.20_spmd, body=%wide.region_17.19_spmd.sunk | while | flops 1379397632 | bytes 71424608 | solution.py:93
  995.0 12.0 copy.182
  1011.8 12.6 fusion.89
  1039.4 12.6 fusion.83
  1062.7 43.4 %all-reduce = (f32[512]{0:T(512)}, f32[512]{0:T(512)}, f32[512]{0:T(512)}, f32[512]{0:T(512)}, f32[512]{0:T(512)}, /*index=5*/f32[512]{0:T(512)}, f32[512]{0:T(512)}, f32[512]{0:T(512)}, f32[2048]{0:T(1024)}, f32[512]{0:T(512)}) all-reduce(f32[512]{0:T(512)S(1)} %get-tuple-element.197, ...), channel_id=1, replica_groups=mesh['task'=4,'feat'=8] {'task','feat'}, use_global_device_ids=true, to_apply=%region_24.25 | all-reduce | flops 6656 | bytes 53248 | tf_op jit(solution)/shard_map/psum | solution.py:234
  1116.5 197.0 %all-reduce.4.cloned.1.call-done = (f32[512,1536]{1,0:T(8,128)}, f32[512,512]{1,0:T(8,128)}, f32[512,1536]{1,0:T(8,128)}, f32[512,512]{1,0:T(8,128)}, f32[512,2048]{1,0:T(8,128)}, /*index=5*/f32[2048,512]{1,0:T(8,128)}) async-done(((f32[512,1536]{1,0:T(8,128)}, f32[512,512]{1,0:T(8,128)}, f32[512,1536]{1,0:T(8,128)}, f32[512,512]{1,0:T(8,128)}, f32[512,2048]{1,0:T(8,128)}, ...) | async-done | bytes 16777232 | tf_op jit(solution)/shard_map/psum | solution.py:234
  (355 shorter events, 537.2 us)
Async XLA Ops:
  7.2 413.7 %copy-start = (bf16[512,2048]{1,0:T(8,128)(2,1)S(1)}, bf16[512,2048]{1,0:T(8,128)(2,1)}, u32[]{:S(2)}) copy-start(bf16[512,2048]{1,0:T(8,128)(2,1)} %param.39) | copy-start | bytes 6291460
  173.6 54.8 %all-to-all-start = ((bf16[1,8,512,512]{3,1,0,2:T(8,128)(2,1)}), bf16[1,8,512,512]{3,1,0,2:T(8,128)(2,1)}, u32[]{:S(2)}, u32[]{:S(2)}) async-start(bf16[1,8,512,512]{3,1,0,2:T(8,128)(2,1)} %copy.152), calls=%async_computation | async-start | bytes 8388608 | tf_op jit(solution)/shard_map/all_to_all | solution.py:150
  228.4 186.6 %all-to-all-start.2 = ((bf16[1,8,512,512]{3,1,0,2:T(8,128)(2,1)}), bf16[1,8,512,512]{3,1,0,2:T(8,128)(2,1)}, u32[]{:S(2)}, u32[]{:S(2)}) async-start(bf16[1,8,512,512]{3,1,0,2:T(8,128)(2,1)} %copy.161), calls=%async_computation.2 | async-start | bytes 8388608 | tf_op jit(solution)/shard_map/all_to_all | solution.py:153
  241.0 12.8 copy-start.25
  246.6 12.7 copy-start.29
  254.5 14.8 %copy-start.37 = (f32[4096]{0:T(1024)}, f32[4096]{0:T(1024)S(1)}, u32[]{:S(2)}) copy-start(f32[4096]{0:T(1024)S(1)} %add.238) | copy-start | bytes 49156
  389.7 11.9 copy-start.24
  389.7 11.9 copy-start.54
  409.0 86.7 %copy-start.31 = (f32[4096]{0:T(1024)}, f32[4096]{0:T(1024)S(1)}, u32[]{:S(2)}) copy-start(f32[4096]{0:T(1024)S(1)} %broadcast_multiply_fusion.1) | copy-start | bytes 49156
  414.2 81.4 %copy-start.43 = (f32[4096]{0:T(1024)}, f32[4096]{0:T(1024)S(1)}, u32[]{:S(2)}) copy-start(f32[4096]{0:T(1024)S(1)} %fusion.74) | copy-start | bytes 49156
  522.8 12.8 copy-start.18
  660.4 32.6 %copy-start.26 = (f32[8,8,64]{2,1,0:T(8,128)S(1)}, f32[8,8,64]{2,1,0:T(8,128)}, u32[]{:S(2)}) copy-start(f32[8,8,64]{2,1,0:T(8,128)} %copy-done.25) | copy-start | bytes 49156
  660.4 32.6 %copy-start.41 = (f32[8,8,64]{2,1,0:T(8,128)S(1)}, f32[8,8,64]{2,1,0:T(8,128)}, u32[]{:S(2)}) copy-start(f32[8,8,64]{2,1,0:T(8,128)} %get-tuple-element.268) | copy-start | bytes 49156
  660.4 32.6 %copy-start.48 = (f32[512]{0:T(512)S(1)}, f32[512]{0:T(512)}, u32[]{:S(2)}) copy-start(f32[512]{0:T(512)} %param.32) | copy-start | bytes 6148
  660.4 32.6 %copy-start.50 = (f32[512]{0:T(512)S(1)}, f32[512]{0:T(512)}, u32[]{:S(2)}) copy-start(f32[512]{0:T(512)} %param.33) | copy-start | bytes 6148
  693.0 10.5 copy-start.30
  693.0 10.5 copy-start.34
  693.0 10.5 copy-start.64
  693.0 26.0 %slice-start = ((s8[8388608]{0:T(1024)(128)(4,1)}), s8[4194304]{0:T(1024)(128)(4,1)S(1)}, s32[]{:S(2)}) async-start(s8[8388608]{0:T(1024)(128)(4,1)} %bitcast.289), calls=%async_computation.5 | async-start | bytes 8388608
  703.5 15.5 %copy-start.38 = (f32[4096]{0:T(1024)S(1)}, f32[4096]{0:T(1024)}, u32[]{:S(2)}) copy-start(f32[4096]{0:T(1024)} %copy-done.37) | copy-start | bytes 49156
  703.5 15.5 %slice-start.1 = ((s8[8388608]{0:T(1024)(128)(4,1)}), s8[4194304]{0:T(1024)(128)(4,1)S(1)}, s32[]{:S(2)}) async-start(s8[8388608]{0:T(1024)(128)(4,1)} %bitcast.289), calls=%async_computation.6 | async-start | bytes 8388608
  736.4 71.0 %all-to-all-start.3 = ((bf16[1,64,64,512]{3,2,0,1:T(8,128)(2,1)}), bf16[1,64,64,512]{3,2,0,1:T(8,128)(2,1)}, u32[]{:S(2)}, u32[]{:S(2)}) async-start(bf16[1,64,64,512]{3,2,0,1:T(8,128)(2,1)} %bitcast.301), calls=%async_computation.3 | async-start | bytes 8388608 | tf_op jit(solution)/shard_map/all_to_all | solution.py:214
  741.2 15.1 %copy-start.62 = (bf16[2048,512]{1,0:T(8,128)(2,1)S(1)}, bf16[2048,512]{1,0:T(8,128)(2,1)}, u32[]{:S(2)}) copy-start(bf16[2048,512]{1,0:T(8,128)(2,1)} %param.41) | copy-start | bytes 6291460
  741.2 15.1 %copy-start.71 = (f32[512]{0:T(512)S(1)}, f32[512]{0:T(512)}, u32[]{:S(2)}) copy-start(f32[512]{0:T(512)} %param.42) | copy-start | bytes 6148
  741.2 49.2 %slice-start.2 = ((s8[8388608]{0:T(1024)(128)(4,1)}), s8[4194304]{0:T(1024)(128)(4,1)S(1)}, s32[]{:S(2)}) async-start(s8[8388608]{0:T(1024)(128)(4,1)} %bitcast.291), calls=%async_computation.7 | async-start | bytes 8388608
  756.3 34.1 %slice-start.3 = ((s8[8388608]{0:T(1024)(128)(4,1)}), s8[4194304]{0:T(1024)(128)(4,1)S(1)}, s32[]{:S(2)}) async-start(s8[8388608]{0:T(1024)(128)(4,1)} %bitcast.291), calls=%async_computation.8 | async-start | bytes 8388608
  774.3 12.7 copy-start.8
  774.3 12.7 copy-start.14
  807.4 226.7 %all-to-all-start.1 = ((bf16[1,64,64,512]{3,2,0,1:T(8,128)(2,1)}), bf16[1,64,64,512]{3,2,0,1:T(8,128)(2,1)}, u32[]{:S(2)}, u32[]{:S(2)}) async-start(bf16[1,64,64,512]{3,2,0,1:T(8,128)(2,1)} %bitcast.308), calls=%async_computation.1 | async-start | bytes 8388608 | tf_op jit(solution)/shard_map/all_to_all | solution.py:176
  812.1 501.4 %all-reduce.4.cloned.1.call-start = ((), (), s32[]{:S(2)}) async-start(), calls=%async_computation.4 | async-start | bytes 33554432 | tf_op jit(solution)/shard_map/psum | solution.py:234
  1011.8 12.6 copy-start.17
  1011.8 12.6 copy-start.16
  (51 other events, 337.0 us)
Sparse Core Ops, SparseCore 0:
  1030.1 283.3 all-reduce.3
where the time goes:
time: 1350 us; the launch traced here: 1330 us
  matrix products  499 us (37%)
  local copies, waits for them, and re-layouts  311 us (23%)
  waiting for transfers between devices  240 us (18%)
  other arithmetic  193 us (14%)
  blocking collectives  43.4 us (3%)
  starting transfers between devices  19.8 us (1%)
  between operations  16.2 us (1%)
    psum x1, waiting for transfers between devices, body(): lax.psum((grad_sample_gain, grad_sample_shift, grad_sample_project, grad_...  197 us
    convert_element_type x3, local copies, waits for them, and re-layouts, branch_backward(): grad_packed.reshape(-1, 3 * full_shape[-1]).astype(jnp.bfloat16)  69.5 us
    unnamed x170, local copies, waits for them, and re-layouts  59.8 us
    dot_general x9, matrix products, attend_back(): jnp.einsum('qche,kche->chqk', grad_mixed, values, preferred_element_type=...  52.1 us
    dot_general x9, matrix products, attend_block(): jnp.einsum('qche,kche->chqk', queries, key_rows, preferred_element_type=j...  47.7 us
    dot_general x9, matrix products, attend_block(): jnp.einsum('chqk,kche->qche', shares, values, preferred_element_type=jnp....  46 us
    psum x1, blocking collectives, body(): lax.psum((grad_sample_gain, grad_sample_shift, grad_sample_project, grad_...  43.4 us
    all_to_all x1, waiting for transfers between devices, body(): lax.all_to_all(after_sample.astype(jnp.bfloat16), 'feat', split_axis=2, c...  42.5 us
  transfers between devices with their start and end apart: 5, of which 2 were waited for; matrix products, arithmetic and copies ran while one was open for 38% of the time, Pallas kernels for 0%

commit v1 on v0

--- a/solution.py
+++ b/solution.py
@@ -6,6 +6,18 @@
 HEADS = 8
 HEAD = 64
 EPSILON = 1e-05
+
+
+def rotated_exchange(x, axis, split, join):
+    ways, here = (lax.axis_size(axis), lax.axis_index(axis))
+    width = x.shape[split] // ways
+    turned = jnp.roll(x, -here * width, axis=split)
+    got = [lax.slice_in_dim(turned, 0, width, axis=split)]
+    for far in range(1, ways):
+        sent = lax.slice_in_dim(turned, far * width, (far + 1) * width, axis=split)
+        got.append(lax.ppermute(sent, axis, [(d, (d + far) % ways) for d in range(ways)]))
+    line = jnp.concatenate(got[::-1], axis=join)
+    return jnp.roll(line, (here + 1) * got[0].shape[join], axis=join)
 
 
 def norm_apply(token_rows, norm_gain, norm_shift):
@@ -147,9 +159,7 @@
     )
     after_sample = (stream_in + sample_branch).reshape(inputs.shape)
     regrouped, grad_result = (
-        lax.all_to_all(
-            after_sample.astype(jnp.bfloat16), "feat", split_axis=2, concat_axis=1, tiled=True
-        ),
+        rotated_exchange(after_sample.astype(jnp.bfloat16), "feat", 2, 1),
         lax.all_to_all(cotangent, "feat", split_axis=2, concat_axis=1, tiled=True),
     )
     middle = regrouped.astype(jnp.float32)

time: 1350 us -> 1380 us (1.022)
  waiting for transfers between devices: 240 us -> 296 us
    ppermute x0 -> x7, waiting for transfers between devices: none -> 75.6 us  [rotated_exchange(): lax.ppermute(sent, axis, [(d, (d + far) % ways) for d in range(ways)])]
    all_to_all x1 -> x0, waiting for transfers between devices: 42.5 us -> none  [body(): lax.all_to_all(after_sample.astype(jnp.bfloat16), 'feat', split_axis=2, c...]
    all_to_all x1, waiting for transfers between devices: 0.01 us -> 22.9 us  [body(): lax.all_to_all(grad_sent, 'feat', split_axis=1, concat_axis=2, tiled=True)]
    unnamed x170 -> x165, local copies, waits for them, and re-layouts: 59.8 us -> 69.1 us
  transfers between devices with their start and end apart: 5 -> 11, of which waited for: 2 -> 7; matrix products, arithmetic and copies ran while one was open for 38% -> 37% of each run, Pallas kernels for 0% -> 0%
where the time goes in v1:
time: 1380 us; the launch traced here: 1370 us
  matrix products  493 us (36%)
  local copies, waits for them, and re-layouts  313 us (23%)
  waiting for transfers between devices  296 us (21%)
  other arithmetic  183 us (13%)
  blocking collectives  42.9 us (3%)
  starting transfers between devices  21.6 us (2%)
  between operations  16.2 us (1%)
    psum x1, waiting for transfers between devices, body(): lax.psum((grad_sample_gain, grad_sample_shift, grad_sample_project, grad_...  197 us
    ppermute x7, waiting for transfers between devices, rotated_exchange(): lax.ppermute(sent, axis, [(d, (d + far) % ways) for d in range(ways)])  75.6 us
    convert_element_type x3, local copies, waits for them, and re-layouts, branch_backward(): grad_packed.reshape(-1, 3 * full_shape[-1]).astype(jnp.bfloat16)  69.6 us
    unnamed x165, local copies, waits for them, and re-layouts  69.1 us
    dot_general x9, matrix products, attend_back(): jnp.einsum('qche,kche->chqk', grad_mixed, values, preferred_element_type=...  51.9 us
    dot_general x9, matrix products, attend_block(): jnp.einsum('qche,kche->chqk', queries, key_rows, preferred_element_type=j...  48.2 us
    dot_general x9, matrix products, attend_block(): jnp.einsum('chqk,kche->qche', shares, values, preferred_element_type=jnp....  46.1 us
    psum x1, blocking collectives, body(): lax.psum((grad_sample_gain, grad_sample_shift, grad_sample_project, grad_...  42.9 us
  transfers between devices with their start and end apart: 11, of which 7 were waited for; matrix products, arithmetic and copies ran while one was open for 37% of the time, Pallas kernels for 0%

profile of v1, /device:TPU:0, one launch (start us, length us, event | category | flops | bytes accessed | tf_op | source)
XLA Modules:
  0.0 1365.8 jit_solution(16253785950127791128)
XLA Ops:
  25.1 16.8 %copy.103 = bf16[4096,1536]{0,1:T(8,128)(2,1)} copy(bf16[4096,1536]{1,0:T(8,128)(2,1)} %convolution_convert_fusion.1) | data formatting | bytes 25165824 | tf_op jit(solution)/shard_map/convert_element_type | solution.py:75
  63.1 79.0 %while.4 = (s32[]{:T(128)}, bf16[8,512,1,8,64]{1,4,3,2,0:T(8,128)(2,1)}, f32[8,1,8,512]{3,2,1,0:T(8,128)}, bf16[8,512,1,8,64]{1,4,3,2,0:T(8,128)(2,1)}, pred[8,5...) while((s32[]{:T(128)}, ...), condition=%wide.region_5.6_spmd, body=%wide.region_2.5_spmd.sunk | while | flops 562294784 | bytes 27399256 | solution.py:81
  207.7 56.0 %collective-permute-done.5 = bf16[1,8,64,512]{3,2,1,0:T(8,128)(2,1)S(1)} collective-permute-done((bf16[1,8,64,512]{3,2,1,0:T(8,128)(2,1)}, bf16[1,8,64,512]{3,2,1,0:T(8,128)(2,1)S(1)}, u32[]{:S(2)}, u32[]{:S(2)}) %collective-permute-start.5) | collective-permute-done | bytes 524320 | tf_op jit(solution)/shard_map/ppermute | solution.py:18
  286.5 30.9 %reshape.546 = bf16[1,64,64,3,8,64]{5,4,3,2,1,0:T(8,128)(2,1)} reshape(bf16[4096,1536]{1,0:T(8,128)(2,1)} %convolution_convert_fusion) | data formatting | bytes 25165824 | tf_op jit(solution)/shard_map/reshape | solution.py:76
  317.5 16.8 %fusion.89 = (bf16[1,64,64,1,8,64]{5,4,3,2,1,0:T(8,128)(2,1)}, bf16[1,64,64,1,8,64]{5,4,3,2,1,0:T(8,128)(2,1)}, bf16[1,64,64,1,8,64]{5,4,3,2,1,0:T(8,128)(2,1)}) fusion(bf16[1,64,64,3,8,64]{5,4,3,2,1,0:T(8,128)(2,1)} %reshape.546), kind=kLoop, calls=%fused_computation.186 | loop fusion | bytes 25165824 | tf_op jit(solution)/shard_map/slice | solution.py:82
  334.3 12.7 copy.153
  346.9 23.1 %multiply_reduce_fusion.2 = (f32[64,8,64]{2,1,0:T(8,128)S(1)}, f32[64,8,64,64]{2,3,1,0:T(8,128)}) fusion(bf16[1,64,64,1,8,64]{5,4,3,2,1,0:T(8,128)(2,1)} %get-tuple-element.246, bf16[1,64,64,1,8,64]{5,4,3,2,1,0:T(8,128)(2,1)} %get-tuple-element.247), kind=kOutput, calls=%fused_computation.82 | convolution fusion | flops 272596992 | bytes 16908288 | tf_op jit(solution)/shard_map/while/body/eval_jaxpr/qche,kche->chqk/dot_general | solution.py:30
  381.2 13.6 convert_bitcast_fusion
  394.9 12.5 copy.112
  441.4 22.3 %multiply_convert_fusion.1 = (bf16[4096,2048]{1,0:T(8,128)(2,1)}, f32[4096,2048]{1,0:T(8,128)}) fusion(f32[2048]{0:T(1024)S(1)} %copy-done.62, bf16[4096,512]{1,0:T(8,128)(2,1)S(1)} %add_convert_fusion.2, bf16[512,2048]{1,0:T(8,128)(2,1)S(1)} %copy-done), kind=kOutput, calls=%fused_computation.71 | convolution fusion | flops 8673820672 | bytes 56631296 | tf_op jit(solution)/shard_map/dot_general | solution.py:179
  465.8 18.4 %fusion.61 = bf16[4096,512]{1,0:T(8,128)(2,1)} fusion(f32[1,64,64,512]{3,2,1,0:T(8,128)} %get-tuple-element.240, bf16[4096,2048]{1,0:T(8,128)(2,1)} %get-tuple-element.273, bf16[2048,512]{1,0:T(8,128)(2,1)} %param.41, f32[512]{0:T(512)S(1)} %copy-done.65), kind=kOutput, calls=%fused_computation.96 | convolution fusion | flops 8596226048 | bytes 31459328 | tf_op jit(solution)/shard_map/dot_general | solution.py:183
  490.1 34.5 %convert_reduce_fusion = (f32[2048]{0:T(1024)}, bf16[4096,2048]{1,0:T(8,128)(2,1)}) fusion(f32[4096,2048]{1,0:T(8,128)} %get-tuple-element.274, f32[2048]{0:T(1024)S(1)} %copy-done.62, bf16[4096,512]{1,0:T(8,128)(2,1)} %bitcast.303, bf16[2048,512]{1,0:T(8,128)(2,1)S(1)} %copy-done.53), kind=kOutput, calls=%fused_computation.70 | convolution fusion | flops 8782870528 | bytes 56639488 | tf_op jit(solution)/shard_map/nd,fd->nf/dot_general | solution.py:197
  524.6 15.4 %fusion.95 = f32[512,2048]{1,0:T(8,128)} fusion(bf16[4096,512]{1,0:T(8,128)(2,1)} %copy-done.21, bf16[4096,2048]{1,0:T(8,128)(2,1)} %get-tuple-element.281), kind=kOutput, calls=%fused_computation.192 | convolution fusion | flops 8589934592 | bytes 25165824 | tf_op jit(solution)/shard_map/nd,nf->df/dot_general | solution.py:201
  540.0 17.1 %multiply_reduce_fusion.3 = (f32[512]{0:T(512)}, f32[4096]{0:T(1024)S(1)}, f32[512]{0:T(512)}, f32[4096,512]{1,0:T(8,128)}) fusion(f32[1,64,64,512]{3,2,1,0:T(8,128)S(1)} %bitcast.299, f32[4096]{0:T(1024)S(1)} %rsqrt.54, f32[4096]{0:T(1024)S(1)} %div.97, f32[512]{0:T(512)S(1)} %copy-done.42, bf16[4096,2048]{1,0:T(8,128)(2,1)} %get-tuple-element.281, ...), kind=kOutput, calls=%fused_computation.106 | convolution fusion | flops 8606707712 | bytes 35706880 | tf_op jit(solution)/shard_map/nf,df->nd/dot_general | solution.py:202
  587.8 12.8 copy.125
  600.6 19.4 %multiply_reduce_fusion.1 = (f32[64,8,64]{2,1,0:T(8,128)S(1)}, f32[64,8,64,64]{2,3,1,0:T(8,128)}) fusion(f32[64,8,64,64]{2,3,1,0:T(8,128)} %get-tuple-element.272, f32[64,8,64]{2,1,0:T(8,128)S(1)} %copy-done.16, bf16[64,64,8,64]{0,3,2,1:T(8,128)(2,1)} %copy.125, bf16[1,64,64,1,8,64]{1,5,4,2,3,0:T(8,128)(2,1)} %copy.153), kind=kOutput, calls=%fused_computation.75 | convolution fusion | flops 276791296 | bytes 25427968 | tf_op jit(solution)/shard_map/while/body/eval_jaxpr/qche,kche->chqk/dot_general | solution.py:54
  620.0 14.9 %multiply_convert_fusion.2 = bf16[64,8,64,64]{2,3,1,0:T(8,128)(2,1)} fusion(f32[64,8,64,64]{2,3,1,0:T(8,128)} %get-tuple-element.277, f32[64,8,64,64]{2,3,1,0:T(8,128)} %get-tuple-element.272, f32[64,8,64]{2,1,0:T(8,128)S(1)} %get-tuple-element.276, f32[64,8,64]{2,1,0:T(8,128)S(1)} %copy-done.16), kind=kLoop, calls=%fused_computation.74 | loop fusion | flops 10485760 | bytes 21233664 | tf_op jit(solution)/shard_map/while/body/eval_jaxpr/convert_element_type | solution.py:58
  634.9 16.1 %multiply_bitcast_fusion.1 = bf16[64,64,1,8,64]{4,0,3,1,2:T(8,128)(2,1)} fusion(bf16[64,8,64,64]{2,3,1,0:T(8,128)(2,1)} %multiply_convert_fusion.2, bf16[1,64,64,1,8,64]{5,4,3,2,1,0:T(8,128)(2,1)} %get-tuple-element.246), kind=kOutput, calls=%fused_computation.73 | convolution fusion | flops 272629760 | bytes 12582912 | tf_op jit(solution)/shard_map/while/body/eval_jaxpr/chqk,kche->qche/dot_general | solution.py:59
  651.0 18.4 %multiply_bitcast_fusion = bf16[64,64,1,8,64]{4,0,3,1,2:T(8,128)(2,1)} fusion(bf16[64,8,64,64]{2,3,1,0:T(8,128)(2,1)} %multiply_convert_fusion.2, bf16[1,64,64,1,8,64]{5,4,3,2,1,0:T(8,128)(2,1)} %get-tuple-element.247), kind=kOutput, calls=%fused_computation.72 | convolution fusion | flops 272629760 | bytes 12582912 | tf_op jit(solution)/shard_map/while/body/eval_jaxpr/chqk,qche->kche/dot_general | solution.py:62
  669.4 13.5 convolution_bitcast_fusion
  682.9 17.4 %maximum_convert_fusion = bf16[64,64,3,8,64]{4,0,3,1,2:T(8,128)(2,1)} fusion(bf16[64,64,1,8,64]{4,0,3,1,2:T(8,128)(2,1)} %convolution_bitcast_fusion, bf16[64,64,1,8,64]{4,0,3,1,2:T(8,128)(2,1)} %multiply_bitcast_fusion, bf16[64,64,1,8,64]{4,0,3,1,2:T(8,128)(2,1)} %multiply_bitcast_fusion.1), kind=kLoop, calls=%fused_computation.60 | loop fusion | flops 12582912 | bytes 25165824 | tf_op jit(solution)/shard_map/convert_element_type | solution.py:116
  700.4 25.0 %copy.128 = bf16[64,64,3,8,64]{4,3,2,1,0:T(8,128)(2,1)} copy(bf16[64,64,3,8,64]{4,0,3,1,2:T(8,128)(2,1)} %maximum_convert_fusion) | data formatting | bytes 25165824 | tf_op jit(solution)/shard_map/convert_element_type | solution.py:116
  725.4 32.6 %convert_element_type.174 = bf16[4096,1536]{1,0:T(8,128)(2,1)} reshape(bf16[64,64,3,8,64]{4,3,2,1,0:T(8,128)(2,1)} %copy.128) | data formatting | bytes 25165824 | tf_op jit(solution)/shard_map/convert_element_type | solution.py:116
  758.0 12.6 fusion.84
  790.3 12.3 fusion.93
  802.6 13.9 %fusion.96 = f32[2048,512]{1,0:T(8,128)} fusion(bf16[4096,2048]{1,0:T(8,128)(2,1)} %get-tuple-element.273, bf16[4096,512]{1,0:T(8,128)(2,1)S(1)} %bitcast.304), kind=kOutput, calls=%fused_computation.193 | convolution fusion | flops 8589934592 | bytes 25165824 | tf_op jit(solution)/shard_map/nf,nd->fd/dot_general | solution.py:196
  816.5 22.9 %all-to-all-done.2 = bf16[1,64,64,512]{3,2,0,1:T(8,128)(2,1)} async-done(((bf16[1,64,64,512]{3,2,0,1:T(8,128)(2,1)}), bf16[1,64,64,512]{3,2,0,1:T(8,128)(2,1)}, u32[]{:S(2)}, u32[]{:S(2)}) %all-to-all-start.2) | async-done | bytes 4194336 | tf_op jit(solution)/shard_map/all_to_all | solution.py:224
  874.3 152.8 %while.5 = (s32[]{:T(128)}, bf16[8,512,1,3,8,64]{1,5,4,3,2,0:T(8,128)(2,1)}, bf16[8,512,1,8,64]{1,4,3,2,0:T(8,128)(2,1)}, pred[8,512]{1,0:T(8,128)(4,1)S(1)}, bf...) while((s32[]{:T(128)}, ...), condition=%wide.region_19.20_spmd, body=%wide.region_17.19_spmd.sunk | while | flops 1379397632 | bytes 71424608 | solution.py:105
  1043.8 12.8 fusion.91
  1071.4 12.6 fusion.85
  1094.6 42.9 %all-reduce = (f32[512]{0:T(512)}, f32[512]{0:T(512)}, f32[512]{0:T(512)}, f32[512]{0:T(512)}, f32[512]{0:T(512)}, /*index=5*/f32[512]{0:T(512)}, f32[512]{0:T(512)}, f32[512]{0:T(512)}, f32[2048]{0:T(1024)}, f32[512]{0:T(512)}) all-reduce(f32[512]{0:T(512)S(1)} %get-tuple-element.182, ...), channel_id=1, replica_groups=mesh['task'=4,'feat'=8] {'task','feat'}, use_global_device_ids=true, to_apply=%region_24.25 | all-reduce | flops 6656 | bytes 53248 | tf_op jit(solution)/shard_map/psum | solution.py:244
  1147.9 197.0 %all-reduce.4.cloned.1.call-done = (f32[512,1536]{1,0:T(8,128)}, f32[512,512]{1,0:T(8,128)}, f32[512,1536]{1,0:T(8,128)}, f32[512,512]{1,0:T(8,128)}, f32[512,2048]{1,0:T(8,128)}, /*index=5*/f32[2048,512]{1,0:T(8,128)}) async-done(((f32[512,1536]{1,0:T(8,128)}, f32[512,512]{1,0:T(8,128)}, f32[512,1536]{1,0:T(8,128)}, f32[512,512]{1,0:T(8,128)}, f32[512,2048]{1,0:T(8,128)}, ...) | async-done | bytes 16777232 | tf_op jit(solution)/shard_map/psum | solution.py:244
  (364 shorter events, 561.6 us)
Async XLA Ops:
  7.2 434.2 %copy-start = (bf16[512,2048]{1,0:T(8,128)(2,1)S(1)}, bf16[512,2048]{1,0:T(8,128)(2,1)}, u32[]{:S(2)}) copy-start(bf16[512,2048]{1,0:T(8,128)(2,1)} %param.39) | copy-start | bytes 6291460
  161.4 12.9 copy-start.17
  168.3 15.9 %collective-permute-start = (bf16[1,8,64,512]{3,2,1,0:T(8,128)(2,1)}, bf16[1,8,64,512]{3,2,1,0:T(8,128)(2,1)S(1)}, u32[]{:S(2)}, u32[]{:S(2)}) collective-permute-start(bf16[1,8,64,512]{3,2,1,0:T(8,128)(2,1)} %get-tuple-element.260), channel_id=1, source_target_pairs={{0,7},{1,0},{2,1},{3,2},{4,3},{5,4},{6,5},{7,6},{8,15},{9,8},{10,9... | collective-permute-start | bytes 1572872 | tf_op jit(solution)/shard_map/ppermute | solution.py:18
  171.6 23.8 %collective-permute-start.1 = (bf16[1,8,64,512]{3,2,1,0:T(8,128)(2,1)}, bf16[1,8,64,512]{3,2,1,0:T(8,128)(2,1)S(1)}, u32[]{:S(2)}, u32[]{:S(2)}) collective-permute-start(bf16[1,8,64,512]{3,2,1,0:T(8,128)(2,1)} %get-tuple-element.259), channel_id=1, source_target_pairs={{0,6},{1,7},{2,0},{3,1},{4,2},{5,3},{6,4},{7,5},{8,14},{9,15},{10,... | collective-permute-start | bytes 1572872 | tf_op jit(solution)/shard_map/ppermute | solution.py:18
  172.2 23.3 %collective-permute-start.2 = (bf16[1,8,64,512]{3,2,1,0:T(8,128)(2,1)}, bf16[1,8,64,512]{3,2,1,0:T(8,128)(2,1)}, u32[]{:S(2)}, u32[]{:S(2)}) collective-permute-start(bf16[1,8,64,512]{3,2,1,0:T(8,128)(2,1)} %get-tuple-element.258), channel_id=1, source_target_pairs={{0,5},{1,6},{2,7},{3,0},{4,1},{5,2},{6,3},{7,4},{8,13},{9,14},{10,... | collective-permute-start | bytes 1572872 | tf_op jit(solution)/shard_map/ppermute | solution.py:18
  172.5 26.3 %collective-permute-start.3 = (bf16[1,8,64,512]{3,2,1,0:T(8,128)(2,1)}, bf16[1,8,64,512]{3,2,1,0:T(8,128)(2,1)}, u32[]{:S(2)}, u32[]{:S(2)}) collective-permute-start(bf16[1,8,64,512]{3,2,1,0:T(8,128)(2,1)} %get-tuple-element.257), channel_id=1, source_target_pairs={{0,4},{1,5},{2,6},{3,7},{4,0},{5,1},{6,2},{7,3},{8,12},{9,13},{10,... | collective-permute-start | bytes 1572872 | tf_op jit(solution)/shard_map/ppermute | solution.py:18
  174.1 32.6 %collective-permute-start.4 = (bf16[1,8,64,512]{3,2,1,0:T(8,128)(2,1)}, bf16[1,8,64,512]{3,2,1,0:T(8,128)(2,1)}, u32[]{:S(2)}, u32[]{:S(2)}) collective-permute-start(bf16[1,8,64,512]{3,2,1,0:T(8,128)(2,1)} %get-tuple-element.256), channel_id=1, source_target_pairs={{0,3},{1,4},{2,5},{3,6},{4,7},{5,0},{6,1},{7,2},{8,11},{9,12},{10,... | collective-permute-start | bytes 1572872 | tf_op jit(solution)/shard_map/ppermute | solution.py:18
  178.7 305.5 %all-to-all-start.1 = ((bf16[1,8,512,512]{3,1,0,2:T(8,128)(2,1)}), bf16[1,8,512,512]{3,1,0,2:T(8,128)(2,1)}, u32[]{:S(2)}, u32[]{:S(2)}) async-start(bf16[1,8,512,512]{3,1,0,2:T(8,128)(2,1)} %copy.115), calls=%async_computation.1 | async-start | bytes 8388608 | tf_op jit(solution)/shard_map/all_to_all | solution.py:163
  184.2 79.6 %collective-permute-start.5 = (bf16[1,8,64,512]{3,2,1,0:T(8,128)(2,1)}, bf16[1,8,64,512]{3,2,1,0:T(8,128)(2,1)S(1)}, u32[]{:S(2)}, u32[]{:S(2)}) collective-permute-start(bf16[1,8,64,512]{3,2,1,0:T(8,128)(2,1)} %get-tuple-element.255), channel_id=1, source_target_pairs={{0,2},{1,3},{2,4},{3,5},{4,6},{5,7},{6,0},{7,1},{8,10},{9,11},{10,... | collective-permute-start | bytes 1572872 | tf_op jit(solution)/shard_map/ppermute | solution.py:18
  195.5 68.4 %collective-permute-start.6 = (bf16[1,8,64,512]{3,2,1,0:T(8,128)(2,1)}, bf16[1,8,64,512]{3,2,1,0:T(8,128)(2,1)S(1)}, u32[]{:S(2)}, u32[]{:S(2)}) collective-permute-start(bf16[1,8,64,512]{3,2,1,0:T(8,128)(2,1)} %get-tuple-element.254), channel_id=1, source_target_pairs={{0,1},{1,2},{2,3},{3,4},{4,5},{5,6},{6,7},{7,0},{8,9},{9,10},{10,1... | collective-permute-start | bytes 1572872 | tf_op jit(solution)/shard_map/ppermute | solution.py:18
  407.4 12.0 copy-start.58
  407.4 12.0 copy-start.64
  441.4 22.3 %copy-start.25 = (f32[64,64]{1,0:T(8,128)S(1)}, f32[64,64]{1,0:T(8,128)}, u32[]{:S(2)}) copy-start(f32[64,64]{1,0:T(8,128)} %copy-done.24) | copy-start | bytes 49156
  441.4 23.0 %copy-start.35 = (f32[64,64]{1,0:T(8,128)S(1)}, f32[64,64]{1,0:T(8,128)}, u32[]{:S(2)}) copy-start(f32[64,64]{1,0:T(8,128)} %get-tuple-element.261) | copy-start | bytes 49156
  441.4 24.4 %copy-start.65 = (f32[512]{0:T(512)S(1)}, f32[512]{0:T(512)}, u32[]{:S(2)}) copy-start(f32[512]{0:T(512)} %param.42) | copy-start | bytes 6148
  484.2 55.8 %slice-start = ((s8[8388608]{0:T(1024)(128)(4,1)}), s8[4194304]{0:T(1024)(128)(4,1)S(1)}, s32[]{:S(2)}) async-start(s8[8388608]{0:T(1024)(128)(4,1)} %bitcast.298), calls=%async_computation.4 | async-start | bytes 8388608
  490.1 49.9 %slice-start.1 = ((s8[8388608]{0:T(1024)(128)(4,1)}), s8[4194304]{0:T(1024)(128)(4,1)S(1)}, s32[]{:S(2)}) async-start(s8[8388608]{0:T(1024)(128)(4,1)} %bitcast.298), calls=%async_computation.5 | async-start | bytes 8388608
  540.0 17.1 %copy-start.32 = (f32[4096]{0:T(1024)S(1)}, f32[4096]{0:T(1024)}, u32[]{:S(2)}) copy-start(f32[4096]{0:T(1024)} %copy-done.31) | copy-start | bytes 49156
  587.8 12.8 copy-start.16
  725.4 32.6 %copy-start.28 = (f32[4096]{0:T(1024)S(1)}, f32[4096]{0:T(1024)}, u32[]{:S(2)}) copy-start(f32[4096]{0:T(1024)} %div.102) | copy-start | bytes 49156
  725.4 32.6 %copy-start.41 = (f32[512]{0:T(512)S(1)}, f32[512]{0:T(512)}, u32[]{:S(2)}) copy-start(f32[512]{0:T(512)} %param.32) | copy-start | bytes 6148
  725.4 32.6 %copy-start.55 = (bf16[512,1536]{1,0:T(8,128)(2,1)S(1)}, bf16[512,1536]{1,0:T(8,128)(2,1)}, u32[]{:S(2)}) copy-start(bf16[512,1536]{1,0:T(8,128)(2,1)} %param.34) | copy-start | bytes 4718596
  758.0 12.6 copy-start.37
  785.6 53.9 %all-to-all-start.2 = ((bf16[1,64,64,512]{3,2,0,1:T(8,128)(2,1)}), bf16[1,64,64,512]{3,2,0,1:T(8,128)(2,1)}, u32[]{:S(2)}, u32[]{:S(2)}) async-start(bf16[1,64,64,512]{3,2,0,1:T(8,128)(2,1)} %bitcast.308), calls=%async_computation.2 | async-start | bytes 8388608 | tf_op jit(solution)/shard_map/all_to_all | solution.py:224
  790.3 12.3 copy-start.9
  839.4 226.9 %all-to-all-start = ((bf16[1,64,64,512]{3,2,0,1:T(8,128)(2,1)}), bf16[1,64,64,512]{3,2,0,1:T(8,128)(2,1)}, u32[]{:S(2)}, u32[]{:S(2)}) async-start(bf16[1,64,64,512]{3,2,0,1:T(8,128)(2,1)} %bitcast.316), calls=%async_computation | async-start | bytes 8388608 | tf_op jit(solution)/shard_map/all_to_all | solution.py:186
  844.1 500.7 %all-reduce.4.cloned.1.call-start = ((), (), s32[]{:S(2)}) async-start(), calls=%async_computation.3 | async-start | bytes 33554432 | tf_op jit(solution)/shard_map/psum | solution.py:244
  1043.8 12.9 copy-start.15
  1043.8 12.9 copy-start.14
  1084.0 10.6 copy-start.10
  1084.0 10.5 copy-start.43
  1084.0 10.5 copy-start.44
  (47 other events, 298.8 us)
Sparse Core Ops, SparseCore 0:
  1062.3 282.5 all-reduce.3
